TPU v7x, 32 devices: a whole 2x2x4 slice. The times are simulated.
32 devices in a mesh: dp: 16 (over z, y, x), mp: 2 (over core).
Axes of the slice: x: 2, y: 2, z: 4, core: 2. Of those that a mesh axis runs over, the one named last changes fastest.
Arguments:
- pixels: bfloat16 [16, 13, 256, 256], P('dp'), may hold values from -6 to 6
- band_count: int32 [16], P('dp'), may hold values from 1 to 13
- wavelengths: int32 [16, 13], P('dp'), may hold values from 40 to 249
- size_class: int32 [16], P('dp'), may hold values from 0 to 2
- token_keep: int32 [16, 256], P('dp'), may hold values 0 or 1
- hyp_attn: float32 [4, 128, 128], replicated, may hold values from -0.75 to 0.75
- hyp_mlp_in: float32 [128, 2048], replicated, may hold values from -0.5 to 0.5
- hyp_mlp_out: float32 [2048, 128], replicated, may hold values from -0.125 to 0.125
- hyp_gain: float32 [2, 128], replicated, may hold values from 0.5 to 1.5
- hyp_shift: float32 [2, 128], replicated, may hold values from -4 to 4
- bias_token: float32 [128], replicated, may hold values from -6 to 6
- kern_weight: float32 [128, 768, 256], P(None, 'dp'), may hold values from -0.009765625 to 0.009765625
- kern_bias: float32 [768, 256], P('dp'), may hold values from -0.125 to 0.125
- patch_bias_weight: float32 [128, 768], replicated, may hold values from -0.5 to 0.5
- norm_gain: float32 [2, 768], replicated, may hold values from 0.5 to 1.5
- norm_shift: float32 [2, 768], replicated, may hold values from -4 to 4
- attn_in: float32 [3, 768, 768], P(None, 'dp', 'mp'), may hold values from -0.21875 to 0.21875
- attn_in_bias: float32 [2, 768], P(None, 'mp'), may hold values from -4 to 4
- attn_out: float32 [768, 768], P('dp', 'mp'), may hold values from -0.625 to 0.625
- attn_out_bias: float32 [768], replicated, may hold values from -4 to 4
- mlp_in: float32 [768, 3072], P('dp', 'mp'), may hold values from -0.21875 to 0.21875
- mlp_in_bias: float32 [3072], P('mp'), may hold values from -4 to 4
- mlp_out: float32 [768, 3072], P('dp', 'mp'), may hold values from -0.109375 to 0.109375
- mlp_out_bias: float32 [768], replicated, may hold values from -4 to 4
- cotangent: bfloat16 [16, 256, 768], P('dp'), may hold values from -6 to 6
Outputs:
- layer_out: bfloat16 [16, 256, 768], P('dp')
- pixel_grad: bfloat16 [16, 13, 256, 256], P('dp')
- grad_hyp_attn: float32 [4, 128, 128], replicated
- grad_hyp_mlp_in: float32 [128, 2048], replicated
- grad_hyp_mlp_out: float32 [2048, 128], replicated
- grad_hyp_gain: float32 [2, 128], replicated
- grad_hyp_shift: float32 [2, 128], replicated
- grad_bias_token: float32 [128], replicated
- grad_kern_weight: float32 [128, 768, 256], P(None, 'dp')
- grad_kern_bias: float32 [768, 256], P('dp')
- grad_patch_bias_weight: float32 [128, 768], replicated
- grad_norm_gain: float32 [2, 768], replicated
- grad_norm_shift: float32 [2, 768], replicated
- grad_attn_in: float32 [3, 768, 768], P(None, 'dp', 'mp')
- grad_attn_in_bias: float32 [2, 768], P(None, 'mp')
- grad_attn_out: float32 [768, 768], P('dp', 'mp')
- grad_attn_out_bias: float32 [768], replicated
- grad_mlp_in: float32 [768, 3072], P('dp', 'mp')
- grad_mlp_in_bias: float32 [3072], P('mp')
- grad_mlp_out: float32 [768, 3072], P('dp', 'mp')
- grad_mlp_out_bias: float32 [768], replicated
Inputs may be any that keep to these rules, and one draw needn't show every extreme that they name: Bands 0 to band_count[s] - 1 of slot s are present.
All inputs are finite; a program needn't handle non-finite values. No bound on the sum of `token_keep` on one device may be relied on, other than what follows from the above.
Results may differ from a plain program's by a relative error of at most 0.013.
Values may be sent and summed in bfloat16 or wider, within the bound.
A program may use at most 192 MiB of HBM per device.

v0:
```python
from functools import partial
import math
import jax
import jax.numpy as jnp
from jax import lax
from jax.sharding import PartitionSpec as P

HEAD_DIM = 64
HYP_HEADS = 4
vit_epsilon = 1e-06
hyper_epsilon = 1e-05


def exact_einsum(pattern, left_side, right_side):
    return jnp.einsum(
        pattern,
        left_side,
        right_side,
        precision=lax.Precision.HIGHEST,
        preferred_element_type=jnp.float32,
    )


def fast_einsum(pattern, left_side, right_side):
    return jnp.einsum(pattern, left_side, right_side, preferred_element_type=jnp.float32)


def norm_rows(values, gain_row, shift_row, epsilon):
    center = values - jnp.mean(values, axis=-1, keepdims=True)
    spread = jnp.mean(center * center, axis=-1, keepdims=True)
    return center * lax.rsqrt(spread + epsilon) * gain_row + shift_row


def exact_gelu(values):
    return jax.nn.gelu(values, approximate=False)


def wave_embedding(wavelengths, model_width):
    half_width = model_width // 2
    frequency = 10000.0 ** (-jnp.arange(half_width, dtype=jnp.float32) * 2.0 / model_width)
    angles = wavelengths.astype(jnp.float32)[..., None] * frequency
    return jnp.concatenate([jnp.sin(angles), jnp.cos(angles)], axis=-1)


def hyper_slot(
    embedding, band_valid, hyp_attn, hyp_mlp_in, hyp_mlp_out, hyp_gain, hyp_shift, bias_token
):
    model_width = embedding.shape[-1]
    sequence = jnp.concatenate([embedding, bias_token[None, :]], axis=0)
    keys_valid = jnp.concatenate([band_valid, jnp.ones((1,), dtype=bool)])
    length = sequence.shape[0]
    head_size = model_width // HYP_HEADS
    query_rows = exact_einsum("te,ef->tf", sequence, hyp_attn[0]).reshape(
        length, HYP_HEADS, head_size
    )
    key_rows = exact_einsum("te,ef->tf", sequence, hyp_attn[1]).reshape(
        length, HYP_HEADS, head_size
    )
    value_rows = exact_einsum("te,ef->tf", sequence, hyp_attn[2]).reshape(
        length, HYP_HEADS, head_size
    )
    scores = exact_einsum("qhd,khd->hqk", query_rows, key_rows) * (1.0 / math.sqrt(head_size))
    scores = jnp.where(keys_valid[None, None, :], scores, -1e30)
    weights = jax.nn.softmax(scores, axis=-1)
    mixed_rows = exact_einsum("hqk,khd->qhd", weights, value_rows).reshape(length, model_width)
    first_rows = norm_rows(
        sequence + exact_einsum("te,ef->tf", mixed_rows, hyp_attn[3]),
        hyp_gain[0],
        hyp_shift[0],
        hyper_epsilon,
    )
    inner_rows = exact_gelu(exact_einsum("te,ef->tf", first_rows, hyp_mlp_in))
    second_rows = norm_rows(
        first_rows + exact_einsum("tf,fe->te", inner_rows, hyp_mlp_out),
        hyp_gain[1],
        hyp_shift[1],
        hyper_epsilon,
    )
    return (second_rows[:-1] + embedding, second_rows[-1])


def hyper_all(
    embed_rows, valid_rows, attn_w, mlp_first, mlp_second, gain_rows, shift_rows, token_row, bias_w
):
    code_vals, tail_rows = jax.vmap(hyper_slot, in_axes=(0, 0, None, None, None, None, None, None))(
        embed_rows, valid_rows, attn_w, mlp_first, mlp_second, gain_rows, shift_rows, token_row
    )
    return (code_vals, exact_einsum("se,ec->sc", tail_rows, bias_w))


def per_device(
    pixels,
    band_count,
    wavelengths,
    size_class,
    token_keep,
    hyp_attn,
    hyp_mlp_in,
    hyp_mlp_out,
    hyp_gain,
    hyp_shift,
    bias_token,
    kern_weight,
    kern_bias,
    patch_bias_weight,
    norm_gain,
    norm_shift,
    attn_in,
    attn_in_bias,
    attn_out,
    attn_out_bias,
    mlp_in,
    mlp_in_bias,
    mlp_out,
    mlp_out_bias,
    cotangent,
):
    slot_count, band_total, row_total, pix_size = pixels.shape
    model_width = norm_gain.shape[1]
    hyper_width = hyp_attn.shape[1]
    tokens = slot_count * row_total
    embedding = wave_embedding(wavelengths, hyper_width)
    band_valid = jnp.arange(band_total)[None, :] < band_count[:, None]
    live_rows = jnp.where(
        size_class == 0,
        row_total * 49 // 256,
        jnp.where(size_class == 1, row_total * 196 // 256, row_total),
    )
    position = jnp.arange(row_total)
    row_valid = position[None, :] < live_rows[:, None]
    key_valid = row_valid & ((token_keep == 1) | (position[None, :] == 0))
    row_scale = row_valid.astype(jnp.float32).reshape(tokens, 1)
    band_mask = band_valid.astype(jnp.bfloat16)[:, :, None, None]
    hyper_local = partial(hyper_all, embedding, band_valid)
    (code_vals, patch_bias), hyper_back = jax.vjp(
        hyper_local,
        hyp_attn,
        hyp_mlp_in,
        hyp_mlp_out,
        hyp_gain,
        hyp_shift,
        bias_token,
        patch_bias_weight,
    )
    code_rows = code_vals.astype(jnp.bfloat16).reshape(slot_count * band_total, hyper_width)
    all_codes = lax.all_gather(code_rows, "dp", axis=0, tiled=True)
    kern_low = kern_weight.astype(jnp.bfloat16)
    local_full = (fast_einsum("ne,ecp->ncp", all_codes, kern_low) + kern_bias).astype(jnp.bfloat16)
    kernel = lax.all_to_all(local_full, "dp", split_axis=0, concat_axis=1, tiled=True)
    kernel = kernel.reshape(slot_count, band_total, model_width, pix_size)
    masked_pixels = pixels * band_mask
    embedded = fast_einsum("sbtp,sbcp->stc", masked_pixels, kernel) + patch_bias[:, None, :]
    embedded = embedded.reshape(tokens, model_width)
    weight_shards = (
        attn_in.astype(jnp.bfloat16),
        attn_out.astype(jnp.bfloat16),
        mlp_in.astype(jnp.bfloat16),
        mlp_out.astype(jnp.bfloat16),
    )
    gathered_in, gathered_out, gathered_up, gathered_down = (
        lax.all_gather(weight_shards[0], "dp", axis=1, tiled=True),
        lax.all_gather(weight_shards[1], "dp", axis=0, tiled=True),
        lax.all_gather(weight_shards[2], "dp", axis=0, tiled=True),
        lax.all_gather(weight_shards[3], "dp", axis=0, tiled=True),
    )
    local_heads = gathered_in.shape[2] // HEAD_DIM
    head_grid = (slot_count, row_total, local_heads, HEAD_DIM)
    score_scale = 1.0 / math.sqrt(HEAD_DIM)
    key_open = key_valid[:, None, None, :]
    norm_one = partial(norm_rows, epsilon=vit_epsilon)
    normed_a, first_back = jax.vjp(norm_one, embedded, norm_gain[0], norm_shift[0])
    normed_a = normed_a.astype(jnp.bfloat16)
    input_bias = jnp.stack([attn_in_bias[0], jnp.zeros_like(attn_in_bias[0]), attn_in_bias[1]])[
        :, None, :
    ]
    projected = (fast_einsum("nd,jde->jne", normed_a, gathered_in) + input_bias).astype(
        jnp.bfloat16
    )
    query_rows = projected[0].reshape(head_grid)
    key_rows = projected[1].reshape(head_grid)
    value_rows = projected[2].reshape(head_grid)
    scores = jnp.where(
        key_open, fast_einsum("sqhd,skhd->shqk", query_rows, key_rows) * score_scale, -1e30
    )
    row_peak = jnp.max(scores, axis=-1, keepdims=True)
    exp_scores = jnp.exp(scores - row_peak)
    prob_total = jnp.sum(exp_scores, axis=-1, keepdims=True)
    log_total = row_peak + jnp.log(prob_total)
    prob_low = (exp_scores / prob_total).astype(jnp.bfloat16)
    context = (
        fast_einsum("shqk,skhd->sqhd", prob_low, value_rows)
        .reshape(tokens, local_heads * HEAD_DIM)
        .astype(jnp.bfloat16)
    )
    head_part = fast_einsum("ne,de->nd", context, gathered_out)
    middle = embedded + lax.psum(head_part, "mp") + attn_out_bias
    normed_b, second_back = jax.vjp(norm_one, middle, norm_gain[1], norm_shift[1])
    normed_b = normed_b.astype(jnp.bfloat16)
    pre_act = fast_einsum("nd,df->nf", normed_b, gathered_up) + mlp_in_bias
    activation, gelu_back = jax.vjp(exact_gelu, pre_act)
    activation = activation.astype(jnp.bfloat16)
    unit_part = fast_einsum("nf,df->nd", activation, gathered_down)
    final_rows = (
        middle + lax.psum(unit_part.astype(jnp.bfloat16), "mp").astype(jnp.float32) + mlp_out_bias
    ) * row_scale
    layer_out = final_rows.astype(jnp.bfloat16).reshape(slot_count, row_total, model_width)
    gathered_in, gathered_out, gathered_up, gathered_down = (
        lax.all_gather(weight_shards[0], "dp", axis=1, tiled=True),
        lax.all_gather(weight_shards[1], "dp", axis=0, tiled=True),
        lax.all_gather(weight_shards[2], "dp", axis=0, tiled=True),
        lax.all_gather(weight_shards[3], "dp", axis=0, tiled=True),
    )
    out_grad = cotangent.reshape(tokens, model_width).astype(jnp.float32) * row_scale
    out_grad_low = out_grad.astype(jnp.bfloat16)
    grad_mlp_out_bias = jnp.sum(out_grad, axis=0)
    grad_down = fast_einsum("nd,nf->df", out_grad_low, activation)
    act_grad = fast_einsum("nd,df->nf", out_grad_low, gathered_down).astype(jnp.bfloat16)
    pre_grad = gelu_back(act_grad.astype(jnp.float32))[0].astype(jnp.bfloat16)
    grad_mlp_in_bias = jnp.sum(pre_grad, axis=0, dtype=jnp.float32)
    grad_up = fast_einsum("nd,nf->df", normed_b, pre_grad)
    second_part = fast_einsum("nf,df->nd", pre_grad, gathered_up)
    middle_in, gain_second, shift_second = second_back(lax.psum(second_part, "mp"))
    middle_grad = out_grad + middle_in
    attended_grad = middle_grad.astype(jnp.bfloat16)
    grad_attn_out_bias = jnp.sum(attended_grad, axis=0, dtype=jnp.float32)
    grad_proj = fast_einsum("nd,ne->de", attended_grad, context)
    context_grad = (
        fast_einsum("nd,de->ne", attended_grad, gathered_out)
        .astype(jnp.bfloat16)
        .reshape(head_grid)
    )
    scores_again = jnp.where(
        key_open, fast_einsum("sqhd,skhd->shqk", query_rows, key_rows) * score_scale, -1e30
    )
    prob_full = jnp.exp(scores_again - log_total)
    prob_grad = fast_einsum("sqhd,skhd->shqk", context_grad, value_rows)
    row_inner = jnp.sum(prob_full * prob_grad, axis=-1, keepdims=True)
    score_grad = (prob_full * (prob_grad - row_inner)).astype(jnp.bfloat16)
    query_grad = fast_einsum("shqk,skhd->sqhd", score_grad, key_rows) * score_scale
    key_grad = fast_einsum("shqk,sqhd->skhd", score_grad, query_rows) * score_scale
    value_grad = fast_einsum("shqk,sqhd->skhd", prob_low, context_grad)
    qkv_grad = (
        jnp.stack([query_grad, key_grad, value_grad])
        .reshape(3, tokens, local_heads * HEAD_DIM)
        .astype(jnp.bfloat16)
    )
    grad_in_bias = jnp.stack(
        [
            jnp.sum(qkv_grad[0], axis=0, dtype=jnp.float32),
            jnp.sum(qkv_grad[2], axis=0, dtype=jnp.float32),
        ]
    )
    grad_in = fast_einsum("nd,jne->jde", normed_a, qkv_grad)
    first_part = fast_einsum("jne,jde->nd", qkv_grad, gathered_in)
    embed_in, gain_first, shift_first = first_back(lax.psum(first_part, "mp"))
    embed_grad = (
        (middle_grad + embed_in).astype(jnp.bfloat16).reshape(slot_count, row_total, model_width)
    )
    patch_bias_grad = jnp.sum(embed_grad, axis=1, dtype=jnp.float32)
    band_float = band_valid.astype(jnp.float32)[:, :, None, None]
    pixel_grad = (fast_einsum("stc,sbcp->sbtp", embed_grad, kernel) * band_float).astype(
        jnp.bfloat16
    )
    kernel_grad = (
        fast_einsum("stc,sbtp->sbcp", embed_grad, masked_pixels)
        .astype(jnp.bfloat16)
        .reshape(slot_count * band_total, model_width, pix_size)
    )
    local_grad = lax.all_to_all(kernel_grad, "dp", split_axis=1, concat_axis=0, tiled=True)
    grad_kern_weight = fast_einsum("ne,ncp->ecp", all_codes, local_grad)
    grad_kern_bias = jnp.sum(local_grad, axis=0, dtype=jnp.float32)
    code_part = fast_einsum("ncp,ecp->ne", local_grad, kern_low)
    grad_attn_in, grad_attn_out, grad_mlp_in, grad_mlp_out = (
        lax.psum_scatter(grad_in, "dp", scatter_dimension=1, tiled=True),
        lax.psum_scatter(grad_proj, "dp", scatter_dimension=0, tiled=True),
        lax.psum_scatter(grad_up, "dp", scatter_dimension=0, tiled=True),
        lax.psum_scatter(grad_down, "dp", scatter_dimension=0, tiled=True),
    )
    norms_gain = jnp.stack([gain_first, gain_second])
    norms_shift = jnp.stack([shift_first, shift_second])
    code_grad = lax.psum_scatter(code_part, "dp", scatter_dimension=0, tiled=True).reshape(
        slot_count, band_total, hyper_width
    )
    local_hyper = hyper_back((code_grad, patch_bias_grad))
    summed = lax.psum(
        (
            local_hyper[0],
            local_hyper[1],
            local_hyper[2],
            local_hyper[3],
            local_hyper[4],
            local_hyper[5],
            local_hyper[6],
            norms_gain,
            norms_shift,
            grad_in_bias,
            grad_attn_out_bias,
            grad_mlp_in_bias,
            grad_mlp_out_bias,
        ),
        "dp",
    )
    hyper_grads = summed[:7]
    others = summed[7:]
    return (
        layer_out,
        pixel_grad,
        hyper_grads[0],
        hyper_grads[1],
        hyper_grads[2],
        hyper_grads[3],
        hyper_grads[4],
        hyper_grads[5],
        grad_kern_weight,
        grad_kern_bias,
        hyper_grads[6],
        others[0],
        others[1],
        grad_attn_in,
        others[2],
        grad_attn_out,
        others[3],
        grad_mlp_in,
        others[4],
        grad_mlp_out,
        others[5],
    )


def solution(mesh):
    return jax.shard_map(
        per_device,
        mesh=mesh,
        in_specs=(
            P("dp", None, None, None),
            P("dp"),
            P("dp", None),
            P("dp"),
            P("dp", None),
            P(),
            P(),
            P(),
            P(),
            P(),
            P(),
            P(None, "dp", None),
            P("dp", None),
            P(),
            P(),
            P(),
            P(None, "dp", "mp"),
            P(None, "mp"),
            P("dp", "mp"),
            P(),
            P("dp", "mp"),
            P("mp"),
            P("dp", "mp"),
            P(),
            P("dp", None, None),
        ),
        out_specs=(
            P("dp", None, None),
            P("dp", None, None, None),
            P(),
            P(),
            P(),
            P(),
            P(),
            P(),
            P(None, "dp", None),
            P("dp", None),
            P(),
            P(),
            P(),
            P(None, "dp", "mp"),
            P(None, "mp"),
            P("dp", "mp"),
            P(),
            P("dp", "mp"),
            P("mp"),
            P("dp", "mp"),
            P(),
        ),
        check_vma=False,
    )
```

profile of v0, /device:TPU:0, one launch (start us, length us, event | category | flops | bytes accessed | tf_op | source)
XLA Modules:
  0.0 1387.8 jit_solution(8111671895934261146)
XLA Ops:
  18.4 42.9 %all-gather = bf16[1,208,128]{2,0,1:T(2,128)(2,1)S(1)} all-gather(bf16[1,13,128]{2,0,1:T(2,128)(2,1)S(1)} %copy.152), channel_id=2, replica_groups=mesh['dp'=16,'mp'=2] {'dp'}, dimensions={1}, use_global_device_ids=true | all-gather | bytes 56576 | tf_op jit(solution)/shard_map/all_gather | solution.py:146
  61.4 3.2 convert_element_type.166
  67.8 4.1 copy.154
  72.0 4.7 all-to-all-start
  79.9 134.4 %all_gather.21 = bf16[768,384]{1,0:T(8,128)(2,1)} all-gather(bf16[48,384]{1,0:T(8,128)(2,1)S(1)} %convert_element_type.177), channel_id=1, replica_groups=mesh['dp'=16,'mp'=2] {'dp'}, dimensions={0}, use_global_device_ids=true | all-gather | bytes 626688 | tf_op jit(solution)/shard_map/all_gather | solution.py:162
  214.3 3.1 copy.155
  220.5 2.3 fusion.29
  230.3 32.6 %all-reduce.21.cloned.1.call-done = f32[256,768]{1,0:T(8,128)} async-done(((f32[256,768]{1,0:T(8,128)}), f32[256,768]{1,0:T(8,128)}) %all-reduce.21.cloned.1.call-update) | async-done | bytes 786448 | tf_op jit(solution)/shard_map/psum | solution.py:196
  266.4 63.8 %all-gather.7.cloned.1.call-done = bf16[768,1536]{1,0:T(8,128)(2,1)} async-done(((bf16[48,1536]{1,0:T(8,128)(2,1)}), bf16[768,1536]{1,0:T(8,128)(2,1)}) %all-gather.7.cloned.1.call-update) | async-done | bytes 2359312 | tf_op jit(solution)/shard_map/all_gather | solution.py:163
  330.2 7.1 multiply_convert_fusion.1
  337.2 57.7 %all-gather.9.cloned.1.call-done = bf16[768,1536]{1,0:T(8,128)(2,1)} async-done(((bf16[48,1536]{1,0:T(8,128)(2,1)}), bf16[768,1536]{1,0:T(8,128)(2,1)}) %all-gather.9.cloned.1.call-update) | async-done | bytes 2359312 | tf_op jit(solution)/shard_map/all_gather | solution.py:164
  394.9 4.6 convert_reduce_fusion.1
  403.6 3.5 convolution_convert_fusion.1
  407.3 13.1 all-reduce.25.cloned.1.call-done
  420.4 2.0 multiply_reduce_fusion.1
  423.7 19.2 %all-reduce.23.cloned.1.call-done = bf16[256,768]{1,0:T(8,128)(2,1)} async-done(((bf16[256,768]{1,0:T(8,128)(2,1)}), bf16[256,768]{1,0:T(8,128)(2,1)}) %all-reduce.23.cloned.1.call-update) | async-done | bytes 393232 | tf_op jit(solution)/shard_map/psum | solution.py:204
  442.8 2.5 fusion.132
  450.7 2.3 convolution_convert_fusion.2
  457.5 3.2 convolution_bitcast_fusion.1
  460.8 20.5 %all-reduce.27.cloned.1.call-done = f32[256,768]{1,0:T(8,128)} async-done(((f32[256,768]{1,0:T(8,128)}), f32[256,768]{1,0:T(8,128)}) %all-reduce.27.cloned.1.call-update) | async-done | bytes 786448 | tf_op jit(solution)/shard_map/psum | solution.py:255
  481.4 2.1 multiply_reduce_fusion.2
  486.9 4.2 convert_bitcast_fusion
  491.0 8.6 copy.169
  499.6 6.8 all-to-all-start.1
  511.2 3.7 convolution_bitcast_fusion
  514.9 6.3 copy.180
  522.0 104.5 %all-to-all-done.1 = bf16[13,768,256]{2,0,1:T(8,128)(2,1)} async-done(((bf16[13,768,256]{2,0,1:T(8,128)(2,1)}), bf16[13,768,256]{2,0,1:T(8,128)(2,1)}, u32[]{:S(2)}, u32[]{:S(2)}) %all-to-all-start.1) | async-done | bytes 5111840 | tf_op jit(solution)/shard_map/all_to_all | solution.py:269
  626.6 5.2 copy.171
  631.8 2.3 copy-done.1
  634.1 4.4 fusion.32
  638.5 61.0 %fusion = f32[16,128]{1,0:T(8,128)S(1)} fusion(f32[208,128]{1,0:T(8,128)S(1)} %fusion.32), kind=kCustom, calls=%all-reduce-scatter | all-reduce-scatter fusion | flops 32769 | bytes 115200
  700.8 3.6 collective-permute-start
  704.4 1.8 collective-permute-start.2
  708.5 2.4 multiply_add_fusion
  714.5 2.1 fusion.97
  716.6 3.0 fusion.67
  725.1 3.1 fusion.125
  729.6 3.1 fusion.49
  733.8 4.2 fusion.18
  738.0 2.5 copy.181
  740.6 4.6 fusion.1
  745.2 6.3 copy.182
  751.5 4.8 copy.170
  758.7 79.2 %all-reduce.13 = (f32[2,128]{1,0:T(2,128)}, f32[2,128]{1,0:T(2,128)}, f32[128]{0:T(128)}, f32[2,768]{1,0:T(2,128)}, f32[2,768]{1,0:T(2,128)}, /*index=5*/f32[2,3...) all-reduce(f32[2,128]{1,0:T(2,128)S(1)} %pad_add_fusion.3, ...), channel_id=1, replica_groups=mesh['dp'=16,'mp'=2] {'dp'}, use_global_device_ids=true, to_apply=%region_33.34 | all-reduce | flops 7552 | bytes 60416 | tf_op jit(solution)/shard_map/psum | solution.py:285
  838.0 125.9 %all-reduce.29.cloned.1.call-done = (f32[4,128,128]{2,1,0:T(8,128)}, f32[128,2048]{1,0:T(8,128)}, f32[2048,128]{1,0:T(8,128)}, f32[128,768]{1,0:T(8,128)}, f32[3,768,384]{2,0,1:T(4,128)}) async-done(((f32[4,128,128]{2,1,0:T(8,128)}, f32[128,2048]{1,0:T(8,128)}, f32[2048,128]{1,0:T(8,128)}, f32[128,768]{1,0:T(8,128)}, f32[3,768,384]{2,0,1:T(4,128)}), (f32[4,128,128]{2,1,0:T(8,128)}, f32[128,2048]{1,0:T(8,128)}, ...) | async-done | bytes 6291472 | tf_op jit(solution)/shard_map/psum | solution.py:285
  965.7 126.9 %reduce-scatter.6.cloned.1.call-done = f32[48,384]{1,0:T(8,128)} async-done(((f32[768,384]{1,0:T(8,128)}), f32[48,384]{1,0:T(8,128)}) %reduce-scatter.6.cloned.1.call-update) | async-done | bytes 73744 | tf_op jit(solution)/shard_map/reduce_scatter | solution.py:275
  1092.6 142.0 %reduce-scatter.8.cloned.1.call-done = f32[48,1536]{1,0:T(8,128)} async-done(((f32[768,1536]{1,0:T(8,128)}), f32[48,1536]{1,0:T(8,128)}) %reduce-scatter.8.cloned.1.call-update) | async-done | bytes 294928 | tf_op jit(solution)/shard_map/reduce_scatter | solution.py:276
  1234.6 141.9 %reduce-scatter.10.cloned.1.call-done = f32[48,1536]{1,0:T(8,128)} async-done(((f32[768,1536]{1,0:T(8,128)}), f32[48,1536]{1,0:T(8,128)}) %reduce-scatter.10.cloned.1.call-update) | async-done | bytes 294928 | tf_op jit(solution)/shard_map/reduce_scatter | solution.py:277
  (423 shorter events, 76.0 us)
Async XLA Ops:
  7.2 8.6 copy-start
  7.2 6.7 copy-start.110
  7.2 8.5 copy-start.114
  7.2 8.5 copy-start.115
  7.2 9.2 copy-start.126
  17.8 46.8 %copy-start.123 = (f32[14]{0:T(128)}, f32[14]{0:T(128)S(1)}, u32[]{:S(2)}) copy-start(f32[14]{0:T(128)S(1)} %multiply_reduce_fusion.8) | copy-start | bytes 172
  18.3 61.1 %copy-start.62 = (f32[1,14,128]{2,1,0:T(8,128)}, f32[1,14,128]{2,1,0:T(8,128)S(1)}, u32[]{:S(2)}) copy-start(f32[1,14,128]{2,1,0:T(8,128)S(1)} %add_bitcast_fusion) | copy-start | bytes 21508
  71.9 6.2 copy-start.59
  71.9 6.9 copy-start.113
  71.9 7.4 copy-start.101
  71.9 7.4 copy-start.102
  71.9 7.5 copy-start.28
  72.0 7.8 copy-start.107
  72.0 142.3 %all-to-all-start = ((bf16[208,48,256]{2,1,0:T(8,128)(2,1)}), bf16[208,48,256]{2,1,0:T(8,128)(2,1)}, u32[]{:S(2)}, u32[]{:S(2)}) async-start(bf16[208,48,256]{2,1,0:T(8,128)(2,1)} %copy.154), calls=%async_computation | async-start | bytes 10223616 | tf_op jit(solution)/shard_map/all_to_all | solution.py:149
  76.7 143.2 %all-gather.5.cloned.1.call-start = ((), (), s32[]{:S(2)}) async-start(), calls=%async_computation.5 | async-start | bytes 1880064 | tf_op jit(solution)/shard_map/all_gather | solution.py:161
  77.5 185.5 %all-reduce.21.cloned.1.call-start = ((), (), s32[]{:S(2)}) async-start(), calls=%async_computation.6 | async-start | bytes 1572864 | tf_op jit(solution)/shard_map/psum | solution.py:196
  78.8 138.5 %copy-start.118 = (bf16[13]{0:T(256)(128)(2,1)}, bf16[13]{0:T(256)(128)(2,1)S(1)}, u32[]{:S(2)}) copy-start(bf16[13]{0:T(256)(128)(2,1)S(1)} %get-tuple-element.189) | copy-start | bytes 82
  79.4 140.5 %copy-start.60 = (f32[768]{0:T(1024)}, f32[768]{0:T(1024)S(1)}, u32[]{:S(2)}) copy-start(f32[768]{0:T(1024)S(1)} %get-tuple-element.192) | copy-start | bytes 9220
  79.4 140.5 %copy-start.77 = (f32[768]{0:T(1024)}, f32[768]{0:T(1024)S(1)}, u32[]{:S(2)}) copy-start(f32[768]{0:T(1024)S(1)} %get-tuple-element.120) | copy-start | bytes 9220
  228.2 102.0 %all-gather.7.cloned.1.call-start = ((), (), s32[]{:S(2)}) async-start(), calls=%async_computation.7 | async-start | bytes 2506752 | tf_op jit(solution)/shard_map/all_gather | solution.py:163
  228.9 166.0 %all-gather.9.cloned.1.call-start = ((), (), s32[]{:S(2)}) async-start(), calls=%async_computation.8 | async-start | bytes 2506752 | tf_op jit(solution)/shard_map/all_gather | solution.py:164
  229.7 190.7 %all-reduce.25.cloned.1.call-start = ((), (), s32[]{:S(2)}) async-start(), calls=%async_computation.10 | async-start | bytes 1572864 | tf_op jit(solution)/shard_map/psum | solution.py:222
  402.2 40.6 %all-reduce.23.cloned.1.call-start = ((), (), s32[]{:S(2)}) async-start(), calls=%async_computation.9 | async-start | bytes 786432 | tf_op jit(solution)/shard_map/psum | solution.py:204
  403.6 16.8 %copy-start.65 = (f32[256]{0:T(256)S(1)}, f32[256]{0:T(256)}, u32[]{:S(2)}) copy-start(f32[256]{0:T(256)} %copy-done.64) | copy-start | bytes 3076
  407.0 35.8 %copy-start.67 = (f32[256]{0:T(256)S(1)}, f32[256]{0:T(256)}, u32[]{:S(2)}) copy-start(f32[256]{0:T(256)} %compare_convert_fusion) | copy-start | bytes 3076
  407.1 74.3 %all-reduce.27.cloned.1.call-start = ((), (), s32[]{:S(2)}) async-start(), calls=%async_computation.11 | async-start | bytes 1572864 | tf_op jit(solution)/shard_map/psum | solution.py:255
  447.1 5.9 copy-start.54
  457.5 23.8 %copy-start.3 = (f32[256,768]{1,0:T(8,128)S(1)}, f32[256,768]{1,0:T(8,128)}, u32[]{:S(2)}) copy-start(f32[256,768]{1,0:T(8,128)} %copy-done.2) | copy-start | bytes 2359300
  457.5 23.8 %copy-start.61 = (f32[768]{0:T(1024)S(1)}, f32[768]{0:T(1024)}, u32[]{:S(2)}) copy-start(f32[768]{0:T(1024)} %copy-done.60) | copy-start | bytes 9220
  457.5 23.8 %copy-start.72 = (f32[256]{0:T(256)S(1)}, f32[256]{0:T(256)}, u32[]{:S(2)}) copy-start(f32[256]{0:T(256)} %copy-done.71) | copy-start | bytes 3076
  499.6 126.9 %all-to-all-start.1 = ((bf16[13,768,256]{2,0,1:T(8,128)(2,1)}), bf16[13,768,256]{2,0,1:T(8,128)(2,1)}, u32[]{:S(2)}, u32[]{:S(2)}) async-start(bf16[13,768,256]{2,0,1:T(8,128)(2,1)} %copy.169), calls=%async_computation.1 | async-start | bytes 12582912 | tf_op jit(solution)/shard_map/all_to_all | solution.py:269
  506.5 457.4 %all-reduce.29.cloned.1.call-start = ((), (), s32[]{:S(2)}) async-start(), calls=%async_computation.15 | async-start | bytes 14942208 | tf_op jit(solution)/shard_map/psum | solution.py:285
  514.9 6.3 copy-start.120
  626.6 7.5 copy-start.5
  634.1 72.1 %copy-start.29 = (f32[128,768]{1,0:T(8,128)S(1)}, f32[128,768]{1,0:T(8,128)}, u32[]{:S(2)}) copy-start(f32[128,768]{1,0:T(8,128)} %param.38) | copy-start | bytes 1179652
  634.1 73.4 %copy-start.95 = (f32[14]{0:T(128)S(1)}, f32[14]{0:T(128)}, u32[]{:S(2)}) copy-start(f32[14]{0:T(128)} %copy-done.94) | copy-start | bytes 172
  634.1 73.4 %copy-start.97 = (f32[128]{0:T(128)S(1)}, f32[128]{0:T(128)}, u32[]{:S(2)}) copy-start(f32[128]{0:T(128)} %copy-done.96) | copy-start | bytes 1540
  634.1 73.4 %copy-start.106 = (f32[14]{0:T(128)S(1)}, f32[14]{0:T(128)}, u32[]{:S(2)}) copy-start(f32[14]{0:T(128)} %copy-done.105) | copy-start | bytes 172
  634.1 74.1 %copy-start.124 = (f32[14]{0:T(128)S(1)}, f32[14]{0:T(128)}, u32[]{:S(2)}) copy-start(f32[14]{0:T(128)} %copy-done.123) | copy-start | bytes 172
  634.1 74.3 %copy-start.46 = (f32[14,2048]{1,0:T(8,128)S(1)}, f32[14,2048]{1,0:T(8,128)}, u32[]{:S(2)}) copy-start(f32[14,2048]{1,0:T(8,128)} %copy-done.45) | copy-start | bytes 344068
  699.5 7.6 collective-permute-start.1
  700.8 6.3 collective-permute-start
  704.4 2.6 collective-permute-start.2
  721.5 371.1 %reduce-scatter.6.cloned.1.call-start = ((), (), s32[]{:S(2)}) async-start(), calls=%async_computation.12 | async-start | bytes 1253376 | tf_op jit(solution)/shard_map/reduce_scatter | solution.py:275
  724.0 510.6 %reduce-scatter.8.cloned.1.call-start = ((), (), s32[]{:S(2)}) async-start(), calls=%async_computation.13 | async-start | bytes 5013504 | tf_op jit(solution)/shard_map/reduce_scatter | solution.py:276
  728.2 648.2 %reduce-scatter.10.cloned.1.call-start = ((), (), s32[]{:S(2)}) async-start(), calls=%async_computation.14 | async-start | bytes 5013504 | tf_op jit(solution)/shard_map/reduce_scatter | solution.py:277
  963.9 414.2 %copy-start.32 = (f32[128,2048]{1,0:T(8,128)S(1)}, f32[128,2048]{1,0:T(8,128)}, u32[]{:S(2)}) copy-start(f32[128,2048]{1,0:T(8,128)} %get-tuple-element.197) | copy-start | bytes 3145732
  965.0 414.1 %copy-start.31 = (f32[2048,128]{1,0:T(8,128)S(1)}, f32[2048,128]{1,0:T(8,128)}, u32[]{:S(2)}) copy-start(f32[2048,128]{1,0:T(8,128)} %get-tuple-element.198) | copy-start | bytes 3145732
  (96 other events, 221.1 us)
Sparse Core Ops, SparseCore 0:
  80.8 105.2 all-gather.4
  228.3 34.5 all-reduce.20
  266.7 63.4 all-gather.6
  333.8 61.0 all-gather.8
  402.3 18.0 all-reduce.24
  423.1 19.6 all-reduce.22
  460.9 20.3 all-reduce.26
  721.6 242.2 all-reduce.28
  969.9 122.6 reduce-scatter.5
  1099.0 135.5 reduce-scatter.7
  1240.3 136.0 reduce-scatter.9
where the time goes:
time: 1400 us; the launch traced here: 1390 us
  waiting for transfers between devices  849 us (61%)
  blocking collectives  318 us (23%)
  matrix products  79.3 us (6%)
  local copies, waits for them, and re-layouts  73.6 us (5%)
  other arithmetic  30.8 us (2%)
  starting transfers between devices  19.3 us (1%)
  between operations  18.5 us (1%)
    reduce_scatter x1, waiting for transfers between devices, per_device(): lax.psum_scatter(grad_up, 'dp', scatter_dimension=0, tiled=True)  142 us
    reduce_scatter x1, waiting for transfers between devices, per_device(): lax.psum_scatter(grad_down, 'dp', scatter_dimension=0, tiled=True)  142 us
    all_gather x1, blocking collectives, per_device(): lax.all_gather(weight_shards[1], 'dp', axis=0, tiled=True)  134 us
    reduce_scatter x1, waiting for transfers between devices, per_device(): lax.psum_scatter(grad_proj, 'dp', scatter_dimension=0, tiled=True)  127 us
    psum x1, waiting for transfers between devices, per_device(): lax.psum((local_hyper[0], local_hyper[1], local_hyper[2], local_hyper[3],...  126 us
    all_to_all x1, waiting for transfers between devices, per_device(): lax.all_to_all(kernel_grad, 'dp', split_axis=1, concat_axis=0, tiled=True)  105 us
    psum x1, blocking collectives, per_device(): lax.psum((local_hyper[0], local_hyper[1], local_hyper[2], local_hyper[3],...  79.2 us
    all_gather x1, waiting for transfers between devices, per_device(): lax.all_gather(weight_shards[2], 'dp', axis=0, tiled=True)  63.8 us
  transfers between devices with their start and end apart: 16, of which 12 were waited for; matrix products, arithmetic and copies ran while one was open for 5% of the time, Pallas kernels for 0%

commit v1 on v0

--- a/solution.py
+++ b/solution.py
@@ -9,6 +9,12 @@
 HYP_HEADS = 4
 vit_epsilon = 1e-06
 hyper_epsilon = 1e-05
+
+
+def swap_blocks(x, name, split, join):
+    parts = jnp.split(x, lax.axis_size(name), axis=split)
+    arrived = lax.all_to_all(jnp.stack(parts), name, 0, 0)
+    return jnp.concatenate(arrived, axis=join)
 
 
 def exact_einsum(pattern, left_side, right_side):
@@ -266,7 +272,7 @@
         .astype(jnp.bfloat16)
         .reshape(slot_count * band_total, model_width, pix_size)
     )
-    local_grad = lax.all_to_all(kernel_grad, "dp", split_axis=1, concat_axis=0, tiled=True)
+    local_grad = swap_blocks(kernel_grad, "dp", 1, 0)
     grad_kern_weight = fast_einsum("ne,ncp->ecp", all_codes, local_grad)
     grad_kern_bias = jnp.sum(local_grad, axis=0, dtype=jnp.float32)
     code_part = fast_einsum("ncp,ecp->ne", local_grad, kern_low)

time: 1400 us -> 1410 us (level)
  local copies, waits for them, and re-layouts: 73.6 us -> 110 us
  waiting for transfers between devices: 849 us -> 829 us
    another operation x5 -> x23, local copies, waits for them, and re-layouts: 1.5 us -> 44 us  [the longest x18 42.5 us: swap_blocks(): arrived = lax.all_to_all(jnp.stack(parts), name, 0, 0)]
    all_to_all x1, waiting for transfers between devices: 105 us -> 82.2 us  [swap_blocks(): arrived = lax.all_to_all(jnp.stack(parts), name, 0, 0)]
    unnamed x267 -> x304, local copies, waits for them, and re-layouts: 34.5 us -> 46.7 us
where the time goes in v1:
time: 1410 us; the launch traced here: 1400 us
  waiting for transfers between devices  829 us (59%)
  blocking collectives  313 us (22%)
  local copies, waits for them, and re-layouts  110 us (8%)
  matrix products  80.3 us (6%)
  other arithmetic  33.2 us (2%)
  between operations  18.5 us (1%)
  starting transfers between devices  18.2 us (1%)
    reduce_scatter x1, waiting for transfers between devices, per_device(): lax.psum_scatter(grad_up, 'dp', scatter_dimension=0, tiled=True)  142 us
    reduce_scatter x1, waiting for transfers between devices, per_device(): lax.psum_scatter(grad_down, 'dp', scatter_dimension=0, tiled=True)  142 us
    all_gather x1, blocking collectives, per_device(): lax.all_gather(weight_shards[1], 'dp', axis=0, tiled=True)  134 us
    psum x1, waiting for transfers between devices, per_device(): lax.psum((local_hyper[0], local_hyper[1], local_hyper[2], local_hyper[3],...  128 us
    reduce_scatter x1, waiting for transfers between devices, per_device(): lax.psum_scatter(grad_proj, 'dp', scatter_dimension=0, tiled=True)  127 us
    all_to_all x1, waiting for transfers between devices, swap_blocks(): arrived = lax.all_to_all(jnp.stack(parts), name, 0, 0)  82.2 us
    psum x1, blocking collectives, per_device(): lax.psum((local_hyper[0], local_hyper[1], local_hyper[2], local_hyper[3],...  79.4 us
    all_gather x1, waiting for transfers between devices, per_device(): lax.all_gather(weight_shards[2], 'dp', axis=0, tiled=True)  63.8 us
  transfers between devices with their start and end apart: 16, of which 12 were waited for; matrix products, arithmetic and copies ran while one was open for 5% of the time, Pallas kernels for 0%

profile of v1, /device:TPU:0, one launch (start us, length us, event | category | flops | bytes accessed | tf_op | source)
XLA Modules:
  0.0 1402.9 jit_solution(11782755426984809266)
XLA Ops:
  18.6 42.9 %all-gather = bf16[1,208,128]{2,0,1:T(2,128)(2,1)S(1)} all-gather(bf16[1,13,128]{2,0,1:T(2,128)(2,1)S(1)} %copy.165), channel_id=2, replica_groups=mesh['dp'=16,'mp'=2] {'dp'}, dimensions={1}, use_global_device_ids=true | all-gather | bytes 56576 | tf_op jit(solution)/shard_map/all_gather | solution.py:152
  61.5 3.2 convert_element_type.166
  67.9 4.1 copy.167
  72.1 4.7 all-to-all-start
  80.0 134.4 %all_gather.21 = bf16[768,384]{1,0:T(8,128)(2,1)} all-gather(bf16[48,384]{1,0:T(8,128)(2,1)S(1)} %convert_element_type.177), channel_id=1, replica_groups=mesh['dp'=16,'mp'=2] {'dp'}, dimensions={0}, use_global_device_ids=true | all-gather | bytes 626688 | tf_op jit(solution)/shard_map/all_gather | solution.py:168
  214.4 3.1 copy.168
  220.7 2.3 fusion.29
  230.4 32.6 %all-reduce.21.cloned.1.call-done = f32[256,768]{1,0:T(8,128)} async-done(((f32[256,768]{1,0:T(8,128)}), f32[256,768]{1,0:T(8,128)}) %all-reduce.21.cloned.1.call-update) | async-done | bytes 786448 | tf_op jit(solution)/shard_map/psum | solution.py:202
  266.5 63.8 %all-gather.7.cloned.1.call-done = bf16[768,1536]{1,0:T(8,128)(2,1)} async-done(((bf16[48,1536]{1,0:T(8,128)(2,1)}), bf16[768,1536]{1,0:T(8,128)(2,1)}) %all-gather.7.cloned.1.call-update) | async-done | bytes 2359312 | tf_op jit(solution)/shard_map/all_gather | solution.py:169
  330.3 7.0 multiply_convert_fusion.1
  337.3 57.7 %all-gather.9.cloned.1.call-done = bf16[768,1536]{1,0:T(8,128)(2,1)} async-done(((bf16[48,1536]{1,0:T(8,128)(2,1)}), bf16[768,1536]{1,0:T(8,128)(2,1)}) %all-gather.9.cloned.1.call-update) | async-done | bytes 2359312 | tf_op jit(solution)/shard_map/all_gather | solution.py:170
  395.0 4.6 convert_reduce_fusion.1
  403.7 3.5 convolution_convert_fusion.1
  407.4 13.1 all-reduce.25.cloned.1.call-done
  423.8 19.2 %all-reduce.23.cloned.1.call-done = bf16[256,768]{1,0:T(8,128)(2,1)} async-done(((bf16[256,768]{1,0:T(8,128)(2,1)}), bf16[256,768]{1,0:T(8,128)(2,1)}) %all-reduce.23.cloned.1.call-update) | async-done | bytes 393232 | tf_op jit(solution)/shard_map/psum | solution.py:210
  443.0 2.5 fusion.132
  450.8 2.3 convolution_convert_fusion.2
  457.6 3.2 convolution_bitcast_fusion.1
  460.9 20.5 %all-reduce.27.cloned.1.call-done = f32[256,768]{1,0:T(8,128)} async-done(((f32[256,768]{1,0:T(8,128)}), f32[256,768]{1,0:T(8,128)}) %all-reduce.27.cloned.1.call-update) | async-done | bytes 786448 | tf_op jit(solution)/shard_map/psum | solution.py:261
  488.8 7.1 slice_bitcast_fusion
  498.0 2.2 copy.196
  500.2 2.2 copy.195
  502.4 2.2 copy.194
  504.6 2.2 copy.193
  508.9 2.2 copy.191
  517.6 2.2 copy.187
  521.9 2.2 copy.185
  545.8 6.8 all-to-all-start.1
  557.2 3.7 convolution_bitcast_fusion
  560.9 6.7 copy.207
  568.5 82.2 %all-to-all-done.1 = bf16[16,13,48,256]{3,2,1,0:T(8,128)(2,1)} async-done(((bf16[16,13,48,256]{3,2,1,0:T(8,128)(2,1)}), bf16[16,13,48,256]{3,2,1,0:T(8,128)(2,1)}, u32[]{:S(2)}, u32[]{:S(2)}) %all-to-all-start.1) | async-done | bytes 5111840 | tf_op jit(solution)/shard_map/all_to_all | solution.py:16
  650.7 7.8 fusion.32
  658.5 56.5 %fusion = f32[16,128]{1,0:T(8,128)S(1)} fusion(f32[208,128]{1,0:T(8,128)S(1)} %fusion.32), kind=kCustom, calls=%all-reduce-scatter | all-reduce-scatter fusion | flops 32769 | bytes 115200
  716.3 3.2 collective-permute-start
  723.7 2.4 multiply_add_fusion
  731.7 3.0 fusion.67
  740.3 3.1 fusion.125
  744.7 3.0 fusion.49
  748.8 4.2 fusion.18
  753.0 2.5 copy.208
  755.6 4.6 fusion.1
  760.2 6.3 copy.209
  766.6 4.0 convert_reduce_fusion
  771.4 79.4 %all-reduce.13 = (f32[2,128]{1,0:T(2,128)}, f32[2,128]{1,0:T(2,128)}, f32[128]{0:T(128)}, f32[2,768]{1,0:T(2,128)}, f32[2,768]{1,0:T(2,128)}, /*index=5*/f32[2,3...) all-reduce(f32[2,128]{1,0:T(2,128)S(1)} %pad_add_fusion.3, ...), channel_id=1, replica_groups=mesh['dp'=16,'mp'=2] {'dp'}, use_global_device_ids=true, to_apply=%region_33.34 | all-reduce | flops 7552 | bytes 60416 | tf_op jit(solution)/shard_map/psum | solution.py:291
  850.8 128.2 %all-reduce.29.cloned.1.call-done = (f32[4,128,128]{2,1,0:T(8,128)}, f32[128,2048]{1,0:T(8,128)}, f32[2048,128]{1,0:T(8,128)}, f32[128,768]{1,0:T(8,128)}, f32[3,768,384]{2,0,1:T(4,128)}) async-done(((f32[4,128,128]{2,1,0:T(8,128)}, f32[128,2048]{1,0:T(8,128)}, f32[2048,128]{1,0:T(8,128)}, f32[128,768]{1,0:T(8,128)}, f32[3,768,384]{2,0,1:T(4,128)}), (f32[4,128,128]{2,1,0:T(8,128)}, f32[128,2048]{1,0:T(8,128)}, ...) | async-done | bytes 6291472 | tf_op jit(solution)/shard_map/psum | solution.py:291
  980.8 126.9 %reduce-scatter.6.cloned.1.call-done = f32[48,384]{1,0:T(8,128)} async-done(((f32[768,384]{1,0:T(8,128)}), f32[48,384]{1,0:T(8,128)}) %reduce-scatter.6.cloned.1.call-update) | async-done | bytes 73744 | tf_op jit(solution)/shard_map/reduce_scatter | solution.py:281
  1107.7 142.0 %reduce-scatter.8.cloned.1.call-done = f32[48,1536]{1,0:T(8,128)} async-done(((f32[768,1536]{1,0:T(8,128)}), f32[48,1536]{1,0:T(8,128)}) %reduce-scatter.8.cloned.1.call-update) | async-done | bytes 294928 | tf_op jit(solution)/shard_map/reduce_scatter | solution.py:282
  1249.7 141.9 %reduce-scatter.10.cloned.1.call-done = f32[48,1536]{1,0:T(8,128)} async-done(((f32[768,1536]{1,0:T(8,128)}), f32[48,1536]{1,0:T(8,128)}) %reduce-scatter.10.cloned.1.call-update) | async-done | bytes 294928 | tf_op jit(solution)/shard_map/reduce_scatter | solution.py:283
  (475 shorter events, 118.8 us)
Async XLA Ops:
  7.2 8.7 copy-start
  7.2 6.7 copy-start.121
  7.2 8.6 copy-start.125
  7.2 8.6 copy-start.126
  7.2 9.3 copy-start.137
  17.9 46.8 %copy-start.134 = (f32[14]{0:T(128)}, f32[14]{0:T(128)S(1)}, u32[]{:S(2)}) copy-start(f32[14]{0:T(128)S(1)} %multiply_reduce_fusion.8) | copy-start | bytes 172
  18.5 61.0 %copy-start.73 = (f32[1,14,128]{2,1,0:T(8,128)}, f32[1,14,128]{2,1,0:T(8,128)S(1)}, u32[]{:S(2)}) copy-start(f32[1,14,128]{2,1,0:T(8,128)S(1)} %add_bitcast_fusion) | copy-start | bytes 21508
  72.1 6.2 copy-start.70
  72.1 6.9 copy-start.124
  72.1 7.4 copy-start.112
  72.1 7.4 copy-start.113
  72.1 7.4 copy-start.26
  72.1 7.8 copy-start.118
  72.1 142.3 %all-to-all-start = ((bf16[208,48,256]{2,1,0:T(8,128)(2,1)}), bf16[208,48,256]{2,1,0:T(8,128)(2,1)}, u32[]{:S(2)}, u32[]{:S(2)}) async-start(bf16[208,48,256]{2,1,0:T(8,128)(2,1)} %copy.167), calls=%async_computation | async-start | bytes 10223616 | tf_op jit(solution)/shard_map/all_to_all | solution.py:155
  76.9 143.2 %all-gather.5.cloned.1.call-start = ((), (), s32[]{:S(2)}) async-start(), calls=%async_computation.5 | async-start | bytes 1880064 | tf_op jit(solution)/shard_map/all_gather | solution.py:167
  77.6 185.4 %all-reduce.21.cloned.1.call-start = ((), (), s32[]{:S(2)}) async-start(), calls=%async_computation.6 | async-start | bytes 1572864 | tf_op jit(solution)/shard_map/psum | solution.py:202
  78.9 138.6 %copy-start.129 = (bf16[13]{0:T(256)(128)(2,1)}, bf16[13]{0:T(256)(128)(2,1)S(1)}, u32[]{:S(2)}) copy-start(bf16[13]{0:T(256)(128)(2,1)S(1)} %get-tuple-element.205) | copy-start | bytes 82
  79.5 140.6 %copy-start.71 = (f32[768]{0:T(1024)}, f32[768]{0:T(1024)S(1)}, u32[]{:S(2)}) copy-start(f32[768]{0:T(1024)S(1)} %get-tuple-element.208) | copy-start | bytes 9220
  79.5 140.6 %copy-start.88 = (f32[768]{0:T(1024)}, f32[768]{0:T(1024)S(1)}, u32[]{:S(2)}) copy-start(f32[768]{0:T(1024)S(1)} %get-tuple-element.120) | copy-start | bytes 9220
  228.3 102.0 %all-gather.7.cloned.1.call-start = ((), (), s32[]{:S(2)}) async-start(), calls=%async_computation.7 | async-start | bytes 2506752 | tf_op jit(solution)/shard_map/all_gather | solution.py:169
  229.0 166.0 %all-gather.9.cloned.1.call-start = ((), (), s32[]{:S(2)}) async-start(), calls=%async_computation.8 | async-start | bytes 2506752 | tf_op jit(solution)/shard_map/all_gather | solution.py:170
  229.8 190.7 %all-reduce.25.cloned.1.call-start = ((), (), s32[]{:S(2)}) async-start(), calls=%async_computation.10 | async-start | bytes 1572864 | tf_op jit(solution)/shard_map/psum | solution.py:228
  402.3 40.6 %all-reduce.23.cloned.1.call-start = ((), (), s32[]{:S(2)}) async-start(), calls=%async_computation.9 | async-start | bytes 786432 | tf_op jit(solution)/shard_map/psum | solution.py:210
  403.7 16.8 %copy-start.76 = (f32[256]{0:T(256)S(1)}, f32[256]{0:T(256)}, u32[]{:S(2)}) copy-start(f32[256]{0:T(256)} %copy-done.75) | copy-start | bytes 3076
  407.1 35.8 %copy-start.78 = (f32[256]{0:T(256)S(1)}, f32[256]{0:T(256)}, u32[]{:S(2)}) copy-start(f32[256]{0:T(256)} %compare_convert_fusion) | copy-start | bytes 3076
  407.2 74.2 %all-reduce.27.cloned.1.call-start = ((), (), s32[]{:S(2)}) async-start(), calls=%async_computation.11 | async-start | bytes 1572864 | tf_op jit(solution)/shard_map/psum | solution.py:261
  457.6 23.8 %copy-start.2 = (f32[256,768]{1,0:T(8,128)S(1)}, f32[256,768]{1,0:T(8,128)}, u32[]{:S(2)}) copy-start(f32[256,768]{1,0:T(8,128)} %copy-done.1) | copy-start | bytes 2359300
  457.6 23.8 %copy-start.72 = (f32[768]{0:T(1024)S(1)}, f32[768]{0:T(1024)}, u32[]{:S(2)}) copy-start(f32[768]{0:T(1024)} %copy-done.71) | copy-start | bytes 9220
  457.6 23.8 %copy-start.83 = (f32[256]{0:T(256)S(1)}, f32[256]{0:T(256)}, u32[]{:S(2)}) copy-start(f32[256]{0:T(256)} %copy-done.82) | copy-start | bytes 3076
  530.6 6.1 copy-start.39
  530.6 6.9 copy-start.38
  545.8 104.8 %all-to-all-start.1 = ((bf16[16,13,48,256]{3,2,1,0:T(8,128)(2,1)}), bf16[16,13,48,256]{3,2,1,0:T(8,128)(2,1)}, u32[]{:S(2)}, u32[]{:S(2)}) async-start(bf16[16,13,48,256]{3,2,1,0:T(8,128)(2,1)} %constant_dynamic-update-slice_fusion), calls=%async_computation.1 | async-start | bytes 10223616 | tf_op jit(solution)/shard_map/all_to_all | solution.py:16
  552.7 426.3 %all-reduce.29.cloned.1.call-start = ((), (), s32[]{:S(2)}) async-start(), calls=%async_computation.15 | async-start | bytes 14942208 | tf_op jit(solution)/shard_map/psum | solution.py:291
  560.9 6.8 copy-start.131
  650.6 70.2 %copy-start.27 = (f32[128,768]{1,0:T(8,128)S(1)}, f32[128,768]{1,0:T(8,128)}, u32[]{:S(2)}) copy-start(f32[128,768]{1,0:T(8,128)} %param.38) | copy-start | bytes 1179652
  650.6 71.9 %copy-start.106 = (f32[14]{0:T(128)S(1)}, f32[14]{0:T(128)}, u32[]{:S(2)}) copy-start(f32[14]{0:T(128)} %copy-done.105) | copy-start | bytes 172
  650.6 71.9 %copy-start.108 = (f32[128]{0:T(128)S(1)}, f32[128]{0:T(128)}, u32[]{:S(2)}) copy-start(f32[128]{0:T(128)} %copy-done.107) | copy-start | bytes 1540
  650.6 71.9 %copy-start.117 = (f32[14]{0:T(128)S(1)}, f32[14]{0:T(128)}, u32[]{:S(2)}) copy-start(f32[14]{0:T(128)} %copy-done.116) | copy-start | bytes 172
  650.6 72.7 %copy-start.135 = (f32[14]{0:T(128)S(1)}, f32[14]{0:T(128)}, u32[]{:S(2)}) copy-start(f32[14]{0:T(128)} %copy-done.134) | copy-start | bytes 172
  650.7 72.9 %copy-start.57 = (f32[14,2048]{1,0:T(8,128)S(1)}, f32[14,2048]{1,0:T(8,128)}, u32[]{:S(2)}) copy-start(f32[14,2048]{1,0:T(8,128)} %copy-done.56) | copy-start | bytes 344068
  715.0 7.2 collective-permute-start.1
  716.3 5.9 collective-permute-start
  719.5 2.6 collective-permute-start.2
  736.6 371.1 %reduce-scatter.6.cloned.1.call-start = ((), (), s32[]{:S(2)}) async-start(), calls=%async_computation.12 | async-start | bytes 1253376 | tf_op jit(solution)/shard_map/reduce_scatter | solution.py:281
  739.2 510.5 %reduce-scatter.8.cloned.1.call-start = ((), (), s32[]{:S(2)}) async-start(), calls=%async_computation.13 | async-start | bytes 5013504 | tf_op jit(solution)/shard_map/reduce_scatter | solution.py:282
  743.4 648.2 %reduce-scatter.10.cloned.1.call-start = ((), (), s32[]{:S(2)}) async-start(), calls=%async_computation.14 | async-start | bytes 5013504 | tf_op jit(solution)/shard_map/reduce_scatter | solution.py:283
  979.0 414.2 %copy-start.43 = (f32[128,2048]{1,0:T(8,128)S(1)}, f32[128,2048]{1,0:T(8,128)}, u32[]{:S(2)}) copy-start(f32[128,2048]{1,0:T(8,128)} %get-tuple-element.213) | copy-start | bytes 3145732
  980.1 414.1 %copy-start.42 = (f32[2048,128]{1,0:T(8,128)S(1)}, f32[2048,128]{1,0:T(8,128)}, u32[]{:S(2)}) copy-start(f32[2048,128]{1,0:T(8,128)} %get-tuple-element.214) | copy-start | bytes 3145732
  (107 other events, 294.0 us)
Sparse Core Ops, SparseCore 0:
  81.0 105.2 all-gather.4
  228.4 34.5 all-reduce.20
  266.8 63.4 all-gather.6
  333.9 61.0 all-gather.8
  402.4 18.0 all-reduce.24
  423.3 19.6 all-reduce.22
  461.0 20.3 all-reduce.26
  736.7 242.2 all-reduce.28
  985.1 122.6 reduce-scatter.5
  1114.1 135.5 reduce-scatter.7
  1255.5 136.0 reduce-scatter.9
